TPU v7x, 256 devices: a whole 4x4x8 slice. The times are simulated.
256 devices in a mesh: seq: 32 (over z, y_lo, core), fsdp: 8 (over x, y_hi).
Axes of the slice: x: 4, y: 4 (y_hi: 2, y_lo: 2; y = y_hi * 2 + y_lo), z: 8, core: 2. Of those that a mesh axis runs over, the one named last changes fastest.
Arguments:
- inputs: bfloat16 [16, 4096, 1536], P('fsdp', 'seq'), may hold values from -6 to 6
- gain: float32 [1536], replicated, may hold values from 0.1 to 1.9
- param: bfloat16 [1536, 3, 1536], P('fsdp'), may hold values from -6 to 6
- cotangent: bfloat16 [16, 4096, 1536], P('fsdp', 'seq'), may hold values from -12 to 12
- noise: bfloat16 [1536, 3, 1536], P('fsdp'), may hold values from -6 to 6
Outputs:
- outputs: bfloat16 [16, 4096, 1536], P('fsdp', 'seq')
- new_param: bfloat16 [1536, 3, 1536], P('fsdp')
All inputs are finite; a program needn't handle non-finite values.
Results may differ from a plain program's by a relative error of at most 0.012.
Values may be sent and summed in bfloat16 or wider, within the bound.
No kernel may reach another device: no remote copies, remote signals or barrier semaphores. Data moves between devices by JAX's collectives and lax.ppermute only.
A program may use at most 128 MiB of HBM per device.

v0:
```python
import math
import jax
import jax.numpy as jnp
from jax import lax
from jax.sharding import PartitionSpec as P

DILATION_STEP = 16


def padded(x, sides, width):
    for axis, dim in sides:
        count, length = (lax.axis_size(axis), x.shape[dim])
        up = [(i, (i + 1) % count) for i in range(count - 1)]
        down = [(j, i) for i, j in up]
        last = lax.slice_in_dim(x, length - width, length, axis=dim)
        first = lax.slice_in_dim(x, 0, width, axis=dim)
        before = lax.ppermute(last, axis, up)
        after = lax.ppermute(first, axis, down)
        x = jnp.concatenate([before, x, after], axis=dim)
    return x


def normalise(values, gain):
    floats = values.astype(jnp.float32)
    factor = lax.rsqrt(jnp.mean(floats * floats, axis=-1, keepdims=True) + 1e-06)
    return jax.nn.gelu(floats * factor * gain).astype(jnp.bfloat16)


def convolve(source_rows, kernel, scale):
    span_length = source_rows.shape[1] - 2 * DILATION_STEP
    total = jnp.zeros((source_rows.shape[0], span_length, kernel.shape[0]), jnp.float32)
    for kernel_tap in range(3):
        input_window = source_rows[
            :, kernel_tap * DILATION_STEP : kernel_tap * DILATION_STEP + span_length, :
        ]
        total = total + lax.dot_general(
            input_window,
            kernel[:, kernel_tap, :],
            (((2,), (1,)), ((), ())),
            preferred_element_type=jnp.float32,
        )
    return total * scale


def shards(inputs, gain, param, cotangent, noise):
    seqs, span_length, width = inputs.shape
    scale = 1.0 / math.sqrt(3.0 * width)
    total_rows = seqs * lax.axis_size("fsdp") * span_length * lax.axis_size("seq")
    eta = math.sqrt(3.0 * width / total_rows)
    hidden_state = normalise(inputs, gain)
    padded_input = padded(hidden_state, (("seq", 1),), DILATION_STEP)
    mixed = convolve(padded_input, lax.all_gather(param, "fsdp", axis=0, tiled=True), scale)
    taps = []
    for kernel_tap in range(3):
        input_window = padded_input[
            :, kernel_tap * DILATION_STEP : kernel_tap * DILATION_STEP + span_length, :
        ]
        taps.append(
            lax.dot_general(
                cotangent,
                input_window,
                (((0, 1), (0, 1)), ((), ())),
                preferred_element_type=jnp.float32,
            )
        )
    term = (jnp.stack(taps, axis=1) * scale).astype(jnp.bfloat16)
    term = lax.optimization_barrier(term)
    share = lax.psum_scatter(
        term.astype(jnp.float32).astype(jnp.bfloat16), "fsdp", scatter_dimension=0, tiled=True
    ).astype(jnp.float32)
    seq_share = lax.psum_scatter(share, "seq", scatter_dimension=0, tiled=True)
    piece_rows = seq_share.shape[0]
    offset = lax.axis_index("seq") * piece_rows
    own_param = lax.dynamic_slice_in_dim(param, offset, piece_rows, 0)
    own_noise = lax.dynamic_slice_in_dim(noise, offset, piece_rows, 0)
    updated = (
        own_param.astype(jnp.float32)
        - eta * seq_share
        + math.sqrt(2.0 * eta) * own_noise.astype(jnp.float32)
    )
    new_param = lax.all_gather(updated.astype(jnp.bfloat16), "seq", axis=0, tiled=True)
    outputs = (inputs.astype(jnp.float32) + mixed).astype(jnp.bfloat16)
    return (outputs, new_param)


def solution(mesh):
    placed = (
        P("fsdp", "seq", None),
        P(),
        P("fsdp", None, None),
        P("fsdp", "seq", None),
        P("fsdp", None, None),
    )
    return jax.shard_map(
        shards,
        mesh=mesh,
        in_specs=placed,
        out_specs=(P("fsdp", "seq", None), P("fsdp", None, None)),
        check_vma=False,
    )
```

profile of v0, /device:TPU:1, one launch (start us, length us, event | category | flops | bytes accessed | tf_op | source)
XLA Modules:
  0.0 720.0 jit_solution(8907818899789513406)
XLA Ops:
  7.2 1.5 fusion.9
  8.8 1.8 fusion.13
  10.6 5.1 collective-permute-start.1
  15.8 1.9 collective-permute-start
  17.7 1.4 convolution_bitcast_fusion.1
  19.2 1.4 convolution_bitcast_fusion
  20.6 1.4 convolution_bitcast_fusion.2
  22.0 7.4 %fusion = bf16[1536,3,1536]{0,2,1:T(8,128)(2,1)} fusion(f32[1536,1,1536]{0,2,1:T(8,128)S(1)} %convolution_bitcast_fusion, f32[1536,1,1536]{0,2,1:T(8,128)S(1)} %convolution_bitcast_fusion.1, f32[1536,1,1536]{0,2,1:T(8,128)S(1)} %convolution_bitcast_fusion.2), kind=kLoop, calls=%fused_computation.1 | loop fusion | flops 28311552 | bytes 42467328 | tf_op jit(solution)/shard_map/convert_element_type | solution.py:66
  29.4 17.9 %copy.33 = bf16[1536,4608]{1,0:T(8,128)(2,1)} copy(bf16[1536,4608]{0,1:T(8,128)(2,1)} %bitcast.49) | data formatting | bytes 28311552
  47.4 174.2 %reduce-scatter.4.cloned.1.call-done = bf16[192,4608]{1,0:T(8,128)(2,1)} async-done(((bf16[1536,4608]{1,0:T(8,128)(2,1)}), bf16[192,4608]{1,0:T(8,128)(2,1)}) %reduce-scatter.4.cloned.1.call-update) | async-done | bytes 1769488
  221.6 4.0 copy.34
  225.5 4.0 copy.24
  229.6 5.2 copy.25
  234.8 0.7 all-gather.3.cloned.1.call-update
  235.6 0.6 dynamic-slice
  236.8 0.9 constant_dynamic-slice_fusion.1
  237.8 236.0 %all-reduce.3.cloned.1.call-done = f32[192,3,1536]{2,1,0:T(4,128)} async-done(((f32[192,3,1536]{2,1,0:T(4,128)}), f32[192,3,1536]{2,1,0:T(4,128)}) %all-reduce.3.cloned.1.call-update) | async-done | bytes 3538960
  473.8 1.6 fusion.21
  475.5 168.2 %all-gather.3.cloned.1.call-done = bf16[1536,3,1536]{2,0,1:T(8,128)(2,1)} async-done(((bf16[192,3,1536]{2,0,1:T(8,128)(2,1)}), bf16[1536,3,1536]{2,0,1:T(8,128)(2,1)}) %all-gather.3.cloned.1.call-update) | async-done | bytes 14155792 | tf_op jit(solution)/shard_map/all_gather | solution.py:52
  643.8 3.7 fusion.1
  647.5 3.8 fusion.2
  651.4 4.8 fusion.8
  656.1 54.1 %all-gather.5.cloned.1.call-done = bf16[192,3,1536]{2,1,0:T(4,128)(2,1)} async-done(((bf16[6,3,1536]{2,1,0:T(4,128)(2,1)}), bf16[192,3,1536]{2,1,0:T(4,128)(2,1)}) %all-gather.5.cloned.1.call-update) | async-done | bytes 1769488 | tf_op jit(solution)/shard_map/all_gather | solution.py:81
  710.2 3.2 copy.27
  (20 shorter events, 0.3 us)
Async XLA Ops:
  7.2 230.6 %copy-start = (bf16[192,3,1536]{2,0,1:T(8,128)(2,1)S(1)}, bf16[192,3,1536]{2,0,1:T(8,128)(2,1)}, u32[]{:S(2)}) copy-start(bf16[192,3,1536]{2,0,1:T(8,128)(2,1)} %param.9) | copy-start | bytes 5308420
  7.2 10.6 %copy-start.1 = (bf16[2,128,1536]{2,1,0:T(8,128)(2,1)S(1)}, bf16[2,128,1536]{2,1,0:T(8,128)(2,1)}, u32[]{:S(2)}) copy-start(bf16[2,128,1536]{2,1,0:T(8,128)(2,1)} %param.8) | copy-start | bytes 2359300
  7.2 214.4 %reduce-scatter.4.cloned.1.call-start = ((), (), s32[]{:S(2)}) async-start(), calls=%async_computation.3 | async-start | bytes 15925248
  10.6 8.5 %collective-permute-start.1 = (bf16[2,16,1536]{2,1,0:T(8,128)(2,1)S(1)}, bf16[2,16,1536]{2,1,0:T(8,128)(2,1)S(1)}, u32[]{:S(2)}, u32[]{:S(2)}) collective-permute-start(bf16[2,16,1536]{2,1,0:T(8,128)(2,1)S(1)} %get-tuple-element.9), channel_id=1, source_target_pairs={{8,0},{16,8},{24,16},{32,24},{40,32},{48,40},{56,48},{64,56},{72,6... | collective-permute-start | bytes 294920 | tf_op jit(solution)/shard_map/ppermute | solution.py:18
  15.8 4.8 collective-permute-start
  47.4 426.5 %all-reduce.3.cloned.1.call-start = ((), (), s32[]{:S(2)}) async-start(), calls=%async_computation.4 | async-start | bytes 9437184
  234.8 0.8 copy-start.3
  234.8 409.0 %all-gather.3.cloned.1.call-start = ((), (), s32[]{:S(2)}) async-start(), calls=%async_computation.1 | async-start | bytes 15925248 | tf_op jit(solution)/shard_map/all_gather | solution.py:52
  235.5 474.7 %all-gather.5.cloned.1.call-start = ((), (), s32[]{:S(2)}) async-start(), calls=%async_computation.2 | async-start | bytes 2433024 | tf_op jit(solution)/shard_map/all_gather | solution.py:81
  647.5 3.8 copy-start.2
Sparse Core Ops, SparseCore 0:
  47.5 174.0 reduce-scatter.3
  234.9 238.9 all-reduce.2
  476.8 166.8 all-gather.2
  646.2 63.9 all-gather.4
where the time goes:
time: 721 us; the launch traced here: 720 us
  waiting for transfers between devices  633 us (88%)
  local copies, waits for them, and re-layouts  36 us (5%)
  matrix products  16.6 us (2%)
  between operations  14.6 us (2%)
  other arithmetic  12.4 us (2%)
  starting transfers between devices  7.23 us (1%)
    unnamed x6, waiting for transfers between devices  411 us
    all_gather x1, waiting for transfers between devices, shards(): lax.all_gather(param, 'fsdp', axis=0, tiled=True)  168 us
    all_gather x1, waiting for transfers between devices, shards(): lax.all_gather(updated.astype(jnp.bfloat16), 'seq', axis=0, tiled=True)  54.1 us
    unnamed x12, local copies, waits for them, and re-layouts  25.8 us
  transfers between devices with their start and end apart: 6, of which 4 were waited for; matrix products, arithmetic and copies ran while one was open for 3% of the time, Pallas kernels for 0%

commit v1 on v0

--- a/solution.py
+++ b/solution.py
@@ -3,6 +3,7 @@
 import jax.numpy as jnp
 from jax import lax
 from jax.sharding import PartitionSpec as P
+from jax.lax import all_to_all, axis_size
 
 DILATION_STEP = 16
 
@@ -43,6 +44,15 @@
 
 
 def shards(inputs, gain, param, cotangent, noise):
+
+    def store_run(panel):
+        return jnp.concatenate(
+            all_to_all(
+                jnp.stack([panel] * axis_size("seq")), axis_name="seq", split_axis=0, concat_axis=0
+            ),
+            axis=0,
+        )
+
     seqs, span_length, width = inputs.shape
     scale = 1.0 / math.sqrt(3.0 * width)
     total_rows = seqs * lax.axis_size("fsdp") * span_length * lax.axis_size("seq")
@@ -78,7 +88,7 @@
         - eta * seq_share
         + math.sqrt(2.0 * eta) * own_noise.astype(jnp.float32)
     )
-    new_param = lax.all_gather(updated.astype(jnp.bfloat16), "seq", axis=0, tiled=True)
+    new_param = store_run(updated.astype(jnp.bfloat16))
     outputs = (inputs.astype(jnp.float32) + mixed).astype(jnp.bfloat16)
     return (outputs, new_param)
 

time: 721 us -> 688 us (0.954)
  waiting for transfers between devices: 633 us -> 590 us
    all_gather x1 -> x0, waiting for transfers between devices: 54.1 us -> none  [shards(): lax.all_gather(updated.astype(jnp.bfloat16), 'seq', axis=0, tiled=True)]
    all_gather x1, waiting for transfers between devices: 168 us -> 178 us  [shards(): lax.all_gather(param, 'fsdp', axis=0, tiled=True)]
    unnamed x6 -> x5, waiting for transfers between devices: 411 us -> 412 us
  transfers between devices with their start and end apart: 6 -> 6, of which waited for: 4 -> 3; matrix products, arithmetic and copies ran while one was open for 3% -> 3% of each run, Pallas kernels for 0% -> 0%
where the time goes in v1:
time: 688 us; the launch traced here: 687 us
  waiting for transfers between devices  590 us (86%)
  local copies, waits for them, and re-layouts  39.6 us (6%)
  matrix products  16.6 us (2%)
  between operations  14.5 us (2%)
  starting transfers between devices  14.2 us (2%)
  other arithmetic  11.7 us (2%)
    unnamed x5, waiting for transfers between devices  412 us
    all_gather x1, waiting for transfers between devices, shards(): lax.all_gather(param, 'fsdp', axis=0, tiled=True)  178 us
    unnamed x12, local copies, waits for them, and re-layouts  24.3 us
  transfers between devices with their start and end apart: 6, of which 3 were waited for; matrix products, arithmetic and copies ran while one was open for 3% of the time, Pallas kernels for 0%

profile of v1, /device:TPU:1, one launch (start us, length us, event | category | flops | bytes accessed | tf_op | source)
XLA Modules:
  0.0 686.5 jit_solution(7450138931573164355)
XLA Ops:
  7.2 1.4 fusion.9
  8.7 1.8 fusion.13
  10.5 5.1 collective-permute-start.1
  15.7 1.9 collective-permute-start
  17.6 1.4 convolution_bitcast_fusion.1
  19.1 1.4 convolution_bitcast_fusion
  20.5 1.4 convolution_bitcast_fusion.2
  21.9 7.4 %fusion = bf16[1536,3,1536]{0,2,1:T(8,128)(2,1)} fusion(f32[1536,1,1536]{0,2,1:T(8,128)S(1)} %convolution_bitcast_fusion, f32[1536,1,1536]{0,2,1:T(8,128)S(1)} %convolution_bitcast_fusion.1, f32[1536,1,1536]{0,2,1:T(8,128)S(1)} %convolution_bitcast_fusion.2), kind=kLoop, calls=%fused_computation.1 | loop fusion | flops 28311552 | bytes 42467328 | tf_op jit(solution)/shard_map/convert_element_type | solution.py:76
  29.3 18.7 %copy.39 = bf16[1536,4608]{1,0:T(8,128)(2,1)} copy(bf16[1536,4608]{0,1:T(8,128)(2,1)} %bitcast.51) | data formatting | bytes 28311552
  48.1 174.2 %reduce-scatter.4.cloned.1.call-done = bf16[192,4608]{1,0:T(8,128)(2,1)} async-done(((bf16[1536,4608]{1,0:T(8,128)(2,1)}), bf16[192,4608]{1,0:T(8,128)(2,1)}) %reduce-scatter.4.cloned.1.call-update) | async-done | bytes 1769488
  222.3 4.0 copy.40
  226.3 2.8 copy.30
  229.1 3.7 copy.31
  234.8 237.2 %all-reduce.3.cloned.1.call-done = f32[192,3,1536]{2,1,0:T(4,128)} async-done(((f32[192,3,1536]{2,1,0:T(4,128)}), f32[192,3,1536]{2,1,0:T(4,128)}) %all-reduce.3.cloned.1.call-update) | async-done | bytes 3538960
  472.0 0.9 constant_dynamic-slice_fusion
  472.9 1.1 fusion.21
  474.0 1.6 stack.14
  475.6 7.0 %all-to-all-start = ((bf16[32,6,3,1536]{3,1,2,0:T(8,128)(2,1)}), bf16[32,6,3,1536]{3,1,2,0:T(8,128)(2,1)}, u32[]{:S(2)}, u32[]{:S(2)}) async-start(bf16[32,6,3,1536]{3,1,2,0:T(8,128)(2,1)} %stack.14), calls=%async_computation | async-start | bytes 4718592 | tf_op jit(solution)/shard_map/all_to_all | solution.py:50
  482.6 177.8 %all-gather.2.cloned.1.call-done = bf16[1536,3,1536]{2,0,1:T(8,128)(2,1)} async-done(((bf16[192,3,1536]{2,0,1:T(8,128)(2,1)}), bf16[1536,3,1536]{2,0,1:T(8,128)(2,1)}) %all-gather.2.cloned.1.call-update) | async-done | bytes 14155792 | tf_op jit(solution)/shard_map/all_gather | solution.py:62
  660.4 3.7 fusion.1
  664.1 3.8 fusion.2
  668.0 4.8 fusion.8
  672.7 3.4 copy.33
  676.1 3.8 reshape.18
  (20 shorter events, 1.5 us)
Async XLA Ops:
  7.2 10.5 %copy-start = (bf16[2,128,1536]{2,1,0:T(8,128)(2,1)S(1)}, bf16[2,128,1536]{2,1,0:T(8,128)(2,1)}, u32[]{:S(2)}) copy-start(bf16[2,128,1536]{2,1,0:T(8,128)(2,1)} %param.8) | copy-start | bytes 2359300
  7.2 215.1 %reduce-scatter.4.cloned.1.call-start = ((), (), s32[]{:S(2)}) async-start(), calls=%async_computation.3 | async-start | bytes 15925248
  10.5 8.5 %collective-permute-start.1 = (bf16[2,16,1536]{2,1,0:T(8,128)(2,1)S(1)}, bf16[2,16,1536]{2,1,0:T(8,128)(2,1)S(1)}, u32[]{:S(2)}, u32[]{:S(2)}) collective-permute-start(bf16[2,16,1536]{2,1,0:T(8,128)(2,1)S(1)} %get-tuple-element.3), channel_id=1, source_target_pairs={{8,0},{16,8},{24,16},{32,24},{40,32},{48,40},{56,48},{64,56},{72,6... | collective-permute-start | bytes 294920 | tf_op jit(solution)/shard_map/ppermute | solution.py:19
  15.7 4.8 collective-permute-start
  48.1 423.9 %all-reduce.3.cloned.1.call-start = ((), (), s32[]{:S(2)}) async-start(), calls=%async_computation.4 | async-start | bytes 9437184
  232.8 0.8 copy-start.3
  232.8 427.6 %all-gather.2.cloned.1.call-start = ((), (), s32[]{:S(2)}) async-start(), calls=%async_computation.2 | async-start | bytes 15925248 | tf_op jit(solution)/shard_map/all_gather | solution.py:62
  475.6 197.2 %all-to-all-start = ((bf16[32,6,3,1536]{3,1,2,0:T(8,128)(2,1)}), bf16[32,6,3,1536]{3,1,2,0:T(8,128)(2,1)}, u32[]{:S(2)}, u32[]{:S(2)}) async-start(bf16[32,6,3,1536]{3,1,2,0:T(8,128)(2,1)} %stack.14), calls=%async_computation | async-start | bytes 4718592 | tf_op jit(solution)/shard_map/all_to_all | solution.py:50
  664.1 3.8 copy-start.2
  672.7 7.2 %copy-start.1 = (bf16[2,128,1536]{2,1,0:T(8,128)(2,1)S(1)}, bf16[2,128,1536]{2,1,0:T(8,128)(2,1)}, u32[]{:S(2)}) copy-start(bf16[2,128,1536]{2,1,0:T(8,128)(2,1)} %param.8) | copy-start | bytes 2359300
Sparse Core Ops, SparseCore 0:
  48.2 174.0 reduce-scatter.3
  232.9 238.9 all-reduce.2
  474.9 185.3 all-gather.1
